TPU v7x, 32 devices: a whole 2x2x4 slice. The times are simulated.
32 devices in a mesh: groups: 2 (over x), feat: 4 (over y, core), sub: 4 (over z).
Axes of the slice: x: 2, y: 2, z: 4, core: 2. Of those that a mesh axis runs over, the one named last changes fastest.
Arguments:
- hidden: bfloat16 [32, 8192], P('groups', 'feat'), parts along dimension 0, may hold values from -400 to 400
- input_norm_gain: bfloat16 [8192], P('feat'), may hold values from 0.25 to 1.75
- query_weight: bfloat16 [8192, 4096], P('feat', 'sub'), may hold values from -1 to 1
- key_weight: bfloat16 [8192, 512], P('feat', 'sub'), may hold values from -1 to 1
- value_weight: bfloat16 [8192, 512], P('feat', 'sub'), may hold values from -0.0625 to 0.0625
- adapter_down_weight: bfloat16 [8192, 512], P('feat'), may hold values from -0.0625 to 0.0625
- adapter_up_weight: bfloat16 [512, 4096], P(None, 'sub'), may hold values from -0.75 to 0.75
- output_weight: bfloat16 [4096, 8192], P('sub', 'feat'), may hold values from -0.09375 to 0.09375
- request_adapter: int32 [8], P('groups'), parts along dimension 0, may hold values from 0 to 7
- stored_owner: int32 [8, 4], P('groups'), parts along dimension 0, may hold values from 0 to 3, as said below
- stored_lengths: int32 [8], P('groups'), parts along dimension 0, may hold values from 2048 to 8192, as said below
- stored_keys: bfloat16 [16, 8192, 512], P(('groups', 'feat'), None, 'sub'), parts along dimension 0, may hold values from -400 to 400
- stored_values: bfloat16 [16, 8192, 512], P(('groups', 'feat'), None, 'sub'), parts along dimension 0, may hold values from -12 to 12
Outputs:
- attn_out: bfloat16 [32, 8192], P(('groups', 'sub'), 'feat'), parts along dimension 0
There are 2 independent parts, one for each index of `groups`. A program takes and returns all parts, laid end to end along the dimension named above; an argument that names none is the same for every part. Nothing has to cross between parts.
Inputs may be any that keep to these rules, and one draw needn't show every extreme that they name: `stored_owner`: for every key-value head no owner holds more than 2 requests, and some owner holds exactly 2. `stored_lengths`: some request has exactly 8192 cached tokens and some exactly 2048.
All inputs are finite; a program needn't handle non-finite values.
Results may differ from a plain program's by a relative error of at most 0.014.
Values may be sent and summed in bfloat16 or wider, within the bound.
No kernel may reach another device: no remote copies, remote signals or barrier semaphores. Data moves between devices by JAX's collectives and lax.ppermute only.
A program may use at most 64 MiB of HBM per device.

v0:
```python
import jax
import jax.numpy as jnp
from jax import lax
from jax.sharding import PartitionSpec as P

MODEL_WIDTH = 8192
ADAPTER_RANK = 64
DRAFT = 4


norm_eps = 1e-05
rope_base = 500000.0


def rotate(values, positions):
    half_dim = values.shape[-1] // 2
    inv_freq = rope_base ** (-(jnp.arange(half_dim, dtype=jnp.float32) * 2.0) / values.shape[-1])
    angles = positions * inv_freq
    cosine = jnp.cos(angles)
    sine = jnp.sin(angles)
    first_half = values[..., :half_dim]
    second_half = values[..., half_dim:]
    return jnp.concatenate(
        [first_half * cosine - second_half * sine, second_half * cosine + first_half * sine],
        axis=-1,
    )


def body(
    hidden,
    input_norm_gain,
    query_weight,
    key_weight,
    value_weight,
    adapter_down_weight,
    adapter_up_weight,
    output_weight,
    request_adapter,
    stored_owner,
    stored_lengths,
    stored_keys,
    stored_values,
):
    feat_count = lax.axis_size("feat")
    my_feat = lax.axis_index("feat")
    my_head = lax.axis_index("sub")
    token_inputs = hidden.shape[0]
    query_cols = query_weight.shape[1]
    head_dim = key_weight.shape[1]
    group_size = query_cols // head_dim
    all_cols = query_cols + 2 * head_dim
    slot_count = stored_keys.shape[0]
    requests = request_adapter.shape[0]
    context = stored_keys.shape[1]
    hidden32 = hidden.astype(jnp.float32)
    squares = lax.psum(jnp.sum(hidden32 * hidden32, axis=1), "feat")
    normalized_hidden = (
        hidden32
        * lax.rsqrt(squares / MODEL_WIDTH + norm_eps)[:, None]
        * input_norm_gain.astype(jnp.float32)[None, :]
    ).astype(jnp.bfloat16)
    owner_col = lax.dynamic_slice_in_dim(stored_owner, my_head, 1, 1)[:, 0]
    req_iota = jnp.arange(requests)
    earlier = req_iota[None, :] < req_iota[:, None]
    same_owner = owner_col[None, :] == owner_col[:, None]
    slot_index = jnp.sum(jnp.logical_and(same_owner, earlier).astype(jnp.int32), axis=1)
    row_of = owner_col * slot_count + slot_index
    all_rows = jnp.arange(feat_count * slot_count)
    matches = row_of[None, :] == all_rows[:, None]
    slot_req = jnp.where(
        jnp.any(matches, axis=1), jnp.sum(jnp.where(matches, req_iota[None, :], 0), axis=1), -1
    )
    my_req = lax.dynamic_slice_in_dim(slot_req, my_feat * slot_count, slot_count, 0)
    draft_iota = jnp.arange(DRAFT)
    slot_tokens = jnp.where(
        slot_req[:, None] >= 0, slot_req[:, None] * DRAFT + draft_iota[None, :], -1
    ).reshape(-1)
    my_slot_tokens = lax.dynamic_slice_in_dim(
        slot_tokens, my_feat * slot_count * DRAFT, slot_count * DRAFT, 0
    )
    tok_iota = jnp.arange(token_inputs)
    tok_adapter = jnp.repeat(request_adapter, DRAFT)
    tok_position = jnp.repeat(stored_lengths, DRAFT) + jnp.tile(draft_iota, requests)
    column_adapter = jnp.arange(adapter_down_weight.shape[1]) // ADAPTER_RANK
    adapter_up_weight32 = adapter_up_weight.astype(jnp.float32)

    def adapter_match_mask(adapter_per_row):
        return column_adapter[None, :] == adapter_per_row[:, None]

    adapter_full = jnp.where(
        adapter_match_mask(tok_adapter),
        jnp.dot(normalized_hidden, adapter_down_weight, preferred_element_type=jnp.float32),
        0.0,
    )
    adapter_token = jnp.sum(adapter_full.reshape(token_inputs, -1, ADAPTER_RANK), axis=1)
    adapter_token = lax.psum(adapter_token, "feat")
    rows_dev = slot_count * DRAFT
    wanted = slot_tokens
    picks = wanted[:, None] == tok_iota[None, :]
    rows_x = jnp.dot(
        picks.astype(jnp.bfloat16), normalized_hidden, preferred_element_type=jnp.float32
    ).astype(jnp.bfloat16)
    adapter_per_row = jnp.where(
        wanted >= 0, jnp.sum(jnp.where(picks, tok_adapter[None, :], 0), axis=1), -1
    )
    query_part = jnp.dot(rows_x, query_weight, preferred_element_type=jnp.float32)
    key_part = jnp.dot(rows_x, key_weight, preferred_element_type=jnp.float32)
    value_part = jnp.dot(rows_x, value_weight, preferred_element_type=jnp.float32)
    sums = lax.psum_scatter(
        jnp.concatenate([query_part, key_part, value_part], axis=1),
        "feat",
        scatter_dimension=0,
        tiled=True,
    )
    selected_rows = my_slot_tokens[:, None] == tok_iota[None, :]
    query_total = sums[:, :query_cols]
    adapter_per_row = jnp.where(
        my_slot_tokens >= 0, jnp.sum(jnp.where(selected_rows, tok_adapter[None, :], 0), axis=1), -1
    )
    adapter_rows = jnp.dot(
        selected_rows.astype(jnp.float32), adapter_token, precision=lax.Precision.HIGHEST
    )
    widened_rows = jnp.where(
        adapter_match_mask(adapter_per_row),
        jnp.tile(adapter_rows, (1, column_adapter.shape[0] // ADAPTER_RANK)),
        0.0,
    )
    query_total = query_total + jnp.dot(
        widened_rows, adapter_up_weight32, precision=lax.Precision.HIGHEST
    )
    positions = jnp.sum(jnp.where(selected_rows, tok_position[None, :], 0), axis=1).astype(
        jnp.float32
    )
    query_rot = rotate(
        query_total.reshape(rows_dev, group_size, head_dim), positions[:, None, None]
    ).reshape(rows_dev, query_cols)
    key_rot = rotate(sums[:, query_cols : query_cols + head_dim], positions[:, None])
    packed = jnp.concatenate([query_rot, key_rot, sums[:, query_cols + head_dim :]], axis=1).astype(
        jnp.bfloat16
    )
    blocks = packed.reshape(slot_count, DRAFT, all_cols)
    query = blocks[:, :, :query_cols].reshape(slot_count, DRAFT, group_size, head_dim)
    key_new = blocks[:, :, query_cols : query_cols + head_dim]
    value_new = blocks[:, :, query_cols + head_dim :]
    slot_lengths = jnp.where(
        my_req >= 0,
        jnp.sum(
            jnp.where(my_req[:, None] == req_iota[None, :], stored_lengths[None, :], 0), axis=1
        ),
        0,
    )
    score_scale = head_dim ** (-0.5)
    cache_scores = (
        jnp.einsum("sdgx,scx->sdgc", query, stored_keys, preferred_element_type=jnp.float32)
        * score_scale
    )
    valid_cache = jnp.arange(context)[None, :] < slot_lengths[:, None]
    cache_scores = jnp.where(valid_cache[:, None, None, :], cache_scores, -1e30)
    new_scores = (
        jnp.einsum("sdgx,sex->sdge", query, key_new, preferred_element_type=jnp.float32)
        * score_scale
    )
    causal = draft_iota[None, :] <= draft_iota[:, None]
    new_scores = jnp.where(causal[None, :, None, :], new_scores, -1e30)
    row_max = jnp.maximum(jnp.max(cache_scores, axis=-1), jnp.max(new_scores, axis=-1))
    cache_exp = jnp.exp(cache_scores - row_max[..., None])
    new_exp = jnp.exp(new_scores - row_max[..., None])
    total = jnp.sum(cache_exp, axis=-1) + jnp.sum(new_exp, axis=-1)
    summed = jnp.einsum(
        "sdgc,scx->sdgx",
        cache_exp.astype(jnp.bfloat16),
        stored_values,
        preferred_element_type=jnp.float32,
    )
    summed = summed + jnp.einsum(
        "sdge,sex->sdgx",
        new_exp.astype(jnp.bfloat16),
        value_new,
        preferred_element_type=jnp.float32,
    )
    attended = (
        (summed / total[..., None]).astype(jnp.bfloat16).reshape(slot_count * DRAFT, query_cols)
    )
    wanted = slot_tokens
    picks = (tok_iota[:, None] == wanted[None, :]).astype(jnp.bfloat16)
    token_rows = jnp.dot(
        picks,
        lax.all_gather(attended, "feat", axis=0, tiled=True),
        preferred_element_type=jnp.float32,
    ).astype(jnp.bfloat16)
    outputs = jnp.dot(token_rows, output_weight, preferred_element_type=jnp.float32)
    return lax.psum_scatter(outputs.astype(jnp.bfloat16), "sub", scatter_dimension=0, tiled=True)


def solution(mesh):
    in_specs = (
        P("groups", "feat"),
        P("feat"),
        P("feat", "sub"),
        P("feat", "sub"),
        P("feat", "sub"),
        P("feat", None),
        P(None, "sub"),
        P("sub", "feat"),
        P("groups"),
        P("groups", None),
        P("groups"),
        P(("groups", "feat"), None, "sub"),
        P(("groups", "feat"), None, "sub"),
    )
    out_specs = P(("groups", "sub"), "feat")
    return jax.shard_map(body, mesh=mesh, in_specs=in_specs, out_specs=out_specs, check_vma=False)
```

profile of v0, /device:TPU:0, one launch (start us, length us, event | category | flops | bytes accessed | tf_op | source)
XLA Modules:
  0.0 105.9 jit_solution(8300614141563593867)
XLA Ops:
  6.5 1.0 dynamic-slice_reduce_fusion
  7.6 0.2 convert_reduce_fusion
  7.7 0.1 fusion.43
  7.9 0.7 convert_element_type.49
  8.6 1.0 fusion.19
  9.6 8.4 %psum.14 = f32[16]{0:T(128)S(1)} all-reduce(f32[16]{0:T(128)S(1)} %fusion.19), channel_id=1, replica_groups=mesh['groups'=2,'feat'=4,'sub'=4] {'feat'}, use_global_device_ids=true, to_apply=%region_5.6 | all-reduce | flops 16 | bytes 128 | tf_op jit(solution)/shard_map/psum | solution.py:56
  18.2 1.1 %convolution_convert_fusion = bf16[32,2048]{1,0:T(8,128)(2,1)S(1)} fusion(bf16[16,2048]{1,0:T(8,128)(2,1)} %param.13, f32[2048]{0:T(1024)S(1)} %convert_element_type.49, f32[16]{0:T(128)S(1)} %add_rsqrt_fusion, s32[32]{0:T(128)S(1)} %select_n.89), kind=kOutput, calls=%fused_computation.5 | convolution fusion | flops 2294272 | bytes 204992 | tf_op jit(solution)/shard_map/dot_general | solution.py:100
  19.2 1.2 %fusion.53 = f32[32,128]{1,0:T(8,128)S(1)} fusion(bf16[32,2048]{1,0:T(8,128)(2,1)S(1)} %convolution_convert_fusion, bf16[2048,128]{1,0:T(8,128)(2,1)} %param.17), kind=kOutput, calls=%fused_computation.92 | convolution fusion | flops 16777216 | bytes 671744 | tf_op jit(solution)/shard_map/dot_general | solution.py:108
  20.5 1.2 %fusion.52 = f32[32,128]{1,0:T(8,128)S(1)} fusion(bf16[32,2048]{1,0:T(8,128)(2,1)S(1)} %convolution_convert_fusion, bf16[2048,128]{1,0:T(8,128)(2,1)} %param.16), kind=kOutput, calls=%fused_computation.91 | convolution fusion | flops 16777216 | bytes 671744 | tf_op jit(solution)/shard_map/dot_general | solution.py:107
  21.8 3.1 %fusion.51 = f32[32,1024]{1,0:T(8,128)S(1)} fusion(bf16[32,2048]{1,0:T(8,128)(2,1)S(1)} %convolution_convert_fusion, bf16[2048,1024]{1,0:T(8,128)(2,1)} %param.15), kind=kOutput, calls=%fused_computation.90 | convolution fusion | flops 134217728 | bytes 4456448 | tf_op jit(solution)/shard_map/dot_general | solution.py:106
  24.8 0.7 pad_maximum_fusion
  25.8 0.4 convolution_select_fusion
  26.3 5.9 %psum.15 = f32[16,64]{1,0:T(8,128)S(1)} all-reduce(f32[16,64]{1,0:T(8,128)S(1)} %reduce_sum.86), channel_id=1, replica_groups=mesh['groups'=2,'feat'=4,'sub'=4] {'feat'}, use_global_device_ids=true, to_apply=%region_9.10 | all-reduce | flops 1024 | bytes 8192 | tf_op jit(solution)/shard_map/psum | solution.py:96
  32.3 0.2 fusion.35
  32.7 0.2 select_reduce_fusion
  33.0 0.2 fusion.46
  33.2 0.1 iota_compare_fusion
  33.4 12.2 %reduce-scatter.2.cloned.1.call-done = f32[8,1280]{1,0:T(8,128)} async-done(((f32[32,1280]{1,0:T(8,128)}), f32[8,1280]{1,0:T(8,128)}) %reduce-scatter.2.cloned.1.call-update) | async-done | bytes 40976 | tf_op jit(solution)/shard_map/reduce_scatter | solution.py:109
  45.7 0.9 subtract_convert_fusion.1
  46.5 1.3 %fusion.12 = f32[8,8,128]{2,0,1:T(8,128)S(1)} fusion(bf16[512,1024]{1,0:T(8,128)(2,1)S(1)} %copy-done.2, f32[8,1280]{1,0:T(8,128)} %reduce-scatter.2.cloned.1.call-done, f32[8,512]{1,0:T(8,128)S(1)} %tile.5, s32[512]{0:T(512)S(1)} %add_select_fusion.1, s32[8]{0:T(128)S(1)} %compare_select_fusion), kind=kOutput, calls=%fused_computation.14 | convolution fusion | flops 50348032 | bytes 1132576 | tf_op jit(solution)/shard_map/dot_general | solution.py:128
  47.9 0.1 subtract_convert_fusion
  48.1 3.9 %fusion.49 = (f32[2,4,8]{2,1,0:T(4,128)S(1)}, f32[2,4,8,8192]{3,2,1,0:T(8,128)S(1)}) fusion(bf16[2,4,8,128]{3,2,1,0:T(8,128)(2,1)S(1)} %bitcast.55, bf16[2,8192,128]{2,1,0:T(8,128)(2,1)} %param.24, pred[2,8192]{1,0:T(4,128)(4,1)S(1)} %iota_compare_fusion), kind=kOutput, calls=%fused_computation.88 | convolution fusion | flops 135790528 | bytes 6324480 | tf_op jit(solution)/shard_map/sdgx,scx->sdgc/dot_general | solution.py:154
  52.0 0.2 fusion.50
  52.2 0.7 slice.48
  52.9 0.2 fusion.28
  53.1 0.5 fusion.4
  53.6 0.8 fusion.13
  54.4 5.2 %all_gather.3 = bf16[32,1024]{1,0:T(8,128)(2,1)S(1)} all-gather(bf16[8,1024]{1,0:T(8,128)(2,1)S(1)} %bitcast.58), channel_id=1, replica_groups=mesh['groups'=2,'feat'=4,'sub'=4] {'feat'}, dimensions={0}, use_global_device_ids=true | all-gather | bytes 81920 | tf_op jit(solution)/shard_map/all_gather | solution.py:188
  59.7 3.6 %convolution_convert_fusion.1 = bf16[16,2048]{1,0:T(8,128)(2,1)} fusion(bf16[1024,2048]{1,0:T(8,128)(2,1)} %param.20, bf16[32,1024]{1,0:T(8,128)(2,1)S(1)} %all_gather.3, s32[32]{0:T(128)S(1)} %select_n.89), kind=kOutput, calls=%fused_computation.6 | convolution fusion | flops 68207104 | bytes 4325504 | tf_op jit(solution)/shard_map/dot_general | solution.py:191
  63.3 0.6 dynamic-slice
  64.5 33.2 %all-reduce.3.cloned.1.call-done = bf16[16,2048]{1,0:T(8,128)(2,1)} async-done(((bf16[16,2048]{1,0:T(8,128)(2,1)}), bf16[16,2048]{1,0:T(8,128)(2,1)}) %all-reduce.3.cloned.1.call-update) | async-done | bytes 65552
  97.7 1.4 %constant_dynamic-slice_fusion = bf16[4,2048]{1,0:T(4,128)(2,1)} fusion(bf16[16,2048]{1,0:T(8,128)(2,1)} %all-reduce.3.cloned.1.call-done, u32[]{:T(128)S(6)} %multiply.13), kind=kLoop, calls=%fused_computation.79 | loop fusion | bytes 32772
  (47 shorter events, 1.4 us)
Async XLA Ops:
  6.5 19.2 %copy-start = (bf16[2048,512]{1,0:T(8,128)(2,1)S(1)}, bf16[2048,512]{1,0:T(8,128)(2,1)}, u32[]{:S(2)}) copy-start(bf16[2048,512]{1,0:T(8,128)(2,1)} %param.18) | copy-start | bytes 6291460
  6.5 39.1 %reduce-scatter.2.cloned.1.call-start = ((), (), s32[]{:S(2)}) async-start(), calls=%async_computation.1 | async-start | bytes 204800 | tf_op jit(solution)/shard_map/reduce_scatter | solution.py:109
  21.7 3.9 %copy-start.4 = (s32[4]{0:T(128)S(1)}, s32[4]{0:T(128)}, u32[]{:S(2)}) copy-start(s32[4]{0:T(128)} %param.21) | copy-start | bytes 52
  21.8 4.0 %copy-start.3 = (bf16[16,2048]{1,0:T(8,128)(2,1)S(1)}, bf16[16,2048]{1,0:T(8,128)(2,1)}, u32[]{:S(2)}) copy-start(bf16[16,2048]{1,0:T(8,128)(2,1)} %param.13) | copy-start | bytes 196612
  24.8 7.7 %copy-start.5 = (s32[4]{0:T(128)S(1)}, s32[4]{0:T(128)}, u32[]{:S(2)}) copy-start(s32[4]{0:T(128)} %param.23) | copy-start | bytes 52
  24.8 21.7 %copy-start.2 = (bf16[512,1024]{1,0:T(8,128)(2,1)S(1)}, bf16[512,1024]{1,0:T(8,128)(2,1)}, u32[]{:S(2)}) copy-start(bf16[512,1024]{1,0:T(8,128)(2,1)} %param.19) | copy-start | bytes 3145732
  25.5 72.2 %all-reduce.3.cloned.1.call-start = ((), (), s32[]{:S(2)}) async-start(), calls=%async_computation.2 | async-start | bytes 131072
  48.0 5.6 %copy-start.1 = (bf16[2,8192,128]{2,1,0:T(8,128)(2,1)S(1)}, bf16[2,8192,128]{2,1,0:T(8,128)(2,1)}, u32[]{:S(2)}) copy-start(bf16[2,8192,128]{2,1,0:T(8,128)(2,1)} %param.25) | copy-start | bytes 12582916
  59.7 3.6 %copy-start.6 = (u32[32]{0:T(128)S(1)}, u32[32]{0:T(128)}, u32[]{:S(2)}) copy-start(u32[32]{0:T(128)} %constant.68) | copy-start | bytes 388
Sparse Core Ops, SparseCore 0:
  25.6 19.9 reduce-scatter.1
  63.4 34.2 all-reduce.2
where the time goes:
time: 107 us; the launch traced here: 106 us
  waiting for transfers between devices  45.5 us (43%)
  blocking collectives  19.5 us (18%)
  matrix products  17.2 us (16%)
  between operations  14.3 us (13%)
  other arithmetic  5.08 us (5%)
  local copies, waits for them, and re-layouts  4.35 us (4%)
    unnamed x3, waiting for transfers between devices  33.2 us
    reduce_scatter x1, waiting for transfers between devices, body(): lax.psum_scatter(jnp.concatenate([query_part, key_part, value_part], axis...  12.2 us
    psum x1, blocking collectives, body(): squares = lax.psum(jnp.sum(hidden32 * hidden32, axis=1), 'feat')  8.39 us
    psum x1, blocking collectives, body(): adapter_token = lax.psum(adapter_token, 'feat')  5.86 us
    all_gather x1, blocking collectives, body(): lax.all_gather(attended, 'feat', axis=0, tiled=True)  5.24 us
    dot_general x1, matrix products, body(): jnp.einsum('sdgx,scx->sdgc', query, stored_keys, preferred_element_type=j...  3.9 us
    dot_general x1, matrix products, body(): jnp.dot(token_rows, output_weight, preferred_element_type=jnp.float32)  3.57 us
    dot_general x1, matrix products, body(): jnp.dot(rows_x, query_weight, preferred_element_type=jnp.float32)  3.05 us
  transfers between devices with their start and end apart: 2, of which 2 were waited for; matrix products, arithmetic and copies ran while one was open for 2% of the time, Pallas kernels for 0%

commit v1 on v0

v1 whole, which is shorter than its diff:
```python
import functools

import jax
import jax.numpy as jnp
from jax import lax
from jax.experimental import pallas as pl
from jax.experimental.pallas import tpu as pltpu
from jax.sharding import PartitionSpec as P

ADAPTER_RANK = 64
DRAFT = 4
LANES = 128
NEG = -1e30

norm_eps = 1e-05
rope_base = 500000.0


def slot_of(owner_ref, head, requests):
    owners = [owner_ref[r, head] for r in range(requests)]
    slots = []
    for r in range(requests):
        slot = jnp.int32(0)
        for earlier in range(r):
            slot = slot + (owners[earlier] == owners[r]).astype(jnp.int32)
        slots.append(slot)
    return owners, slots


def project_kernel(
    n_feat,
    slot_count,
    requests,
    chunks,
    owner_ref,
    adapter_ref,
    lengths_ref,
    hidden_ref,
    gain_ref,
    wq_hbm,
    wk_hbm,
    wv_hbm,
    wd_hbm,
    *rest,
):
    out_refs = rest[:n_feat]
    rot_ref = rest[n_feat]
    wq, wk, wv, wd, acc, sems = rest[n_feat + 1 :]
    features = hidden_ref.shape[1]
    step = features // chunks
    pairs = ((wq_hbm, wq), (wk_hbm, wk), (wv_hbm, wv), (wd_hbm, wd))
    copies = []
    for c in range(chunks):
        at = pl.ds(c * step, step)
        copies.append(
            [
                pltpu.make_async_copy(src.at[at], dst.at[at], sems.at[c, i])
                for i, (src, dst) in enumerate(pairs)
            ]
        )
        for copy in copies[-1]:
            copy.start()
    me = lax.axis_index("feat")
    head = lax.axis_index("sub")
    tokens = hidden_ref.shape[0]
    rows_dev = slot_count * DRAFT
    rows = n_feat * rows_dev
    query_cols = wq.shape[1]
    head_dim = wk.shape[1]
    owners, slots = slot_of(owner_ref, head, requests)
    row = lax.broadcasted_iota(jnp.int32, (rows, tokens), 0)
    col = lax.broadcasted_iota(jnp.int32, (rows, tokens), 1)
    row1 = lax.broadcasted_iota(jnp.int32, (rows, 1), 0)
    wanted = jnp.full((rows, tokens), -1, jnp.int32)
    adapter = jnp.full((rows, 1), -1, jnp.int32)
    pos_row = lax.broadcasted_iota(jnp.int32, (rows_dev, LANES), 0)
    position = jnp.zeros((rows_dev, LANES), jnp.int32)
    for r in range(requests):
        block = (owners[r] ^ me) * slot_count + slots[r]
        wanted = jnp.where(row // DRAFT == block, r * DRAFT + row % DRAFT, wanted)
        adapter = jnp.where(row1 // DRAFT == block, adapter_ref[r], adapter)
        position = jnp.where(
            pos_row // DRAFT == block, lengths_ref[r] + pos_row % DRAFT, position
        )
    picks = jnp.where(wanted == col, 1.0, 0.0).astype(jnp.bfloat16)
    picked = jnp.dot(picks, hidden_ref[...], preferred_element_type=jnp.float32)
    squares = jnp.sum(picked * picked, axis=1, keepdims=True)
    x = (picked * gain_ref[...].astype(jnp.float32)).astype(jnp.bfloat16)
    lane = lax.broadcasted_iota(jnp.int32, (rows_dev, LANES), 1)
    half = head_dim // 2
    freq = jnp.exp(
        (lane % half).astype(jnp.float32) * (-2.0 / head_dim * jnp.log(jnp.float32(rope_base)))
    )
    angle = position.astype(jnp.float32) * freq
    sine = jnp.sin(angle)
    rot_ref[:, :LANES] = jnp.cos(angle)
    rot_ref[:, LANES:] = jnp.where(lane < half, -sine, sine)
    starts = (0, query_cols, query_cols + head_dim, query_cols + 2 * head_dim)
    for c in range(chunks):
        part = x[:, c * step : (c + 1) * step]
        for i, (_, w) in enumerate(pairs):
            copies[c][i].wait()
            here = slice(starts[i], starts[i] + w.shape[1])
            term = jnp.dot(
                part, w[c * step : (c + 1) * step, :], preferred_element_type=jnp.float32
            )
            if c == 0:
                acc[:, here] = term
            else:
                acc[:, here] += term
    down = acc[:, starts[3] :]
    dcol = lax.broadcasted_iota(jnp.int32, down.shape, 1)
    down = jnp.where(dcol // ADAPTER_RANK == adapter, down, 0.0)
    mid = down[:, :LANES]
    for t in range(1, down.shape[1] // LANES):
        mid = mid + down[:, t * LANES : (t + 1) * LANES]
    squares = jnp.broadcast_to(squares, (rows, LANES))
    for k in range(n_feat):
        at = slice(k * rows_dev, (k + 1) * rows_dev)
        out_refs[k][:, : starts[3]] = acc[at, : starts[3]]
        out_refs[k][:, starts[3] : starts[3] + LANES] = mid[at]
        out_refs[k][:, starts[3] + LANES :] = squares[at]


def attend_kernel(
    n_feat,
    slot_count,
    requests,
    width,
    chunks,
    owner_ref,
    adapter_ref,
    lengths_ref,
    rot_ref,
    *rest,
):
    part_refs = rest[:n_feat]
    up_hbm, keys_hbm, values_hbm, out_ref, up, keys, values, scores, sems, up_sems = rest[n_feat:]
    context, head_dim = keys.shape[1:]
    step = context // chunks
    me = lax.axis_index("feat")
    head = lax.axis_index("sub")
    rows_dev = slot_count * DRAFT
    query_cols = out_ref.shape[1]
    group = query_cols // head_dim
    owners, slots = slot_of(owner_ref, head, requests)
    slot_adapter = [jnp.int32(0)] * slot_count
    slot_length = [jnp.int32(0)] * slot_count
    for r in range(requests):
        for s in range(slot_count):
            mine = jnp.logical_and(owners[r] == me, slots[r] == s)
            slot_adapter[s] = jnp.where(mine, adapter_ref[r], slot_adapter[s])
            slot_length[s] = jnp.where(mine, lengths_ref[r], slot_length[s])
    per = LANES // ADAPTER_RANK
    up_copies = []
    for s in range(slot_count):
        start = pl.multiple_of(slot_adapter[s] // per * LANES, LANES)
        up_copies.append(
            pltpu.make_async_copy(up_hbm.at[pl.ds(start, LANES)], up.at[s], up_sems.at[s])
        )
        up_copies[-1].start()
    copies = []
    for i, (src, dst) in enumerate(((keys_hbm, keys), (values_hbm, values))):
        for c in range(chunks):
            at = pl.ds(c * step, step)
            copy = pltpu.make_async_copy(src.at[:, at], dst.at[:, at], sems.at[i, c])
            copy.start()
            copies.append(copy)
    total = part_refs[0][...]
    for ref in part_refs[1:]:
        total = total + ref[...]
    base = query_cols + 2 * head_dim
    scale = lax.rsqrt(total[:, base + LANES :] / width + norm_eps)
    row = lax.broadcasted_iota(jnp.int32, (rows_dev, 1), 0)
    mid = total[:, base : base + LANES] * scale
    mid_hi = mid.astype(jnp.bfloat16)
    rest1 = mid - mid_hi.astype(jnp.float32)
    mid_lo = rest1.astype(jnp.bfloat16)
    both = jnp.concatenate([mid_hi, mid_lo], axis=0)
    delta = jnp.zeros((rows_dev, query_cols), jnp.float32)
    for s in range(slot_count):
        up_copies[s].wait()
        d = jnp.dot(both, up[s], preferred_element_type=jnp.float32)
        delta = jnp.where(row // DRAFT == s, d[:rows_dev] + d[rows_dev:], delta)
    cosine = rot_ref[:, :LANES]
    sine = rot_ref[:, LANES:]
    half = head_dim // 2

    def rotate(v):
        return v * cosine + pltpu.roll(v, half, 1) * sine

    plain = []
    wide = []
    for g in range(group):
        at = slice(g * head_dim, (g + 1) * head_dim)
        q = rotate(total[:, at] * scale + delta[:, at])
        plain.append(q)
        wide.append(
            jnp.concatenate(
                [jnp.where(row // DRAFT == s, q, 0.0) for s in range(slot_count)], axis=1
            )
        )
    plain = jnp.concatenate(plain, axis=0).astype(jnp.bfloat16)
    wide = jnp.concatenate(wide, axis=0).astype(jnp.bfloat16)
    key_new = rotate(total[:, query_cols : query_cols + head_dim] * scale).astype(jnp.bfloat16)
    value_new = (total[:, query_cols + head_dim : base] * scale).astype(jnp.bfloat16)
    q_rows = group * rows_dev
    nt = (((1,), (1,)), ((), ()))
    score_scale = head_dim ** (-0.5)
    new = lax.dot_general(plain, key_new, nt, preferred_element_type=jnp.float32) * score_scale
    nrow = lax.broadcasted_iota(jnp.int32, new.shape, 0) % rows_dev
    ncol = lax.broadcasted_iota(jnp.int32, new.shape, 1)
    seen = jnp.logical_and(nrow // DRAFT == ncol // DRAFT, ncol <= nrow)
    new = jnp.where(seen, new, NEG)
    qrow = lax.broadcasted_iota(jnp.int32, (q_rows, 1), 0) % rows_dev
    length = jnp.zeros((q_rows, 1), jnp.int32)
    for s in range(slot_count):
        length = jnp.where(qrow // DRAFT == s, slot_length[s], length)
    peak = jnp.full((q_rows, LANES), NEG, jnp.float32)
    for c in range(chunks):
        copies[c].wait()
        at = slice(c * step, (c + 1) * step)
        kc = jnp.concatenate([keys[s, at] for s in range(slot_count)], axis=1)
        sc = lax.dot_general(wide, kc, nt, preferred_element_type=jnp.float32) * score_scale
        col = lax.broadcasted_iota(jnp.int32, sc.shape, 1) + c * step
        sc = jnp.where(col < length, sc, NEG)
        scores[:, at] = sc
        for t in range(step // LANES):
            peak = jnp.maximum(peak, sc[:, t * LANES : (t + 1) * LANES])
    top = jnp.maximum(jnp.max(peak, axis=1, keepdims=True), jnp.max(new, axis=1, keepdims=True))
    new_e = jnp.exp(new - top)
    acc_sum = jnp.zeros((q_rows, LANES), jnp.float32)
    acc = jnp.zeros((q_rows, slot_count * head_dim), jnp.float32)
    for c in range(chunks):
        copies[chunks + c].wait()
        at = slice(c * step, (c + 1) * step)
        e = jnp.exp(scores[:, at] - top)
        for t in range(step // LANES):
            acc_sum = acc_sum + e[:, t * LANES : (t + 1) * LANES]
        vc = jnp.concatenate([values[s, at] for s in range(slot_count)], axis=1)
        acc = acc + jnp.dot(e.astype(jnp.bfloat16), vc, preferred_element_type=jnp.float32)
    summed = jnp.zeros((q_rows, head_dim), jnp.float32)
    for s in range(slot_count):
        summed = jnp.where(
            qrow // DRAFT == s, acc[:, s * head_dim : (s + 1) * head_dim], summed
        )
    summed = summed + jnp.dot(
        new_e.astype(jnp.bfloat16), value_new, preferred_element_type=jnp.float32
    )
    denom = jnp.sum(acc_sum, axis=1, keepdims=True) + jnp.sum(new_e, axis=1, keepdims=True)
    attended = summed / denom
    for g in range(group):
        out_ref[:, g * head_dim : (g + 1) * head_dim] = attended[
            g * rows_dev : (g + 1) * rows_dev
        ].astype(jnp.bfloat16)


def output_kernel(n_feat, n_sub, slot_count, requests, chunks, owner_ref, *rest):
    att_refs = rest[:n_feat]
    w_hbm = rest[n_feat]
    out_refs = rest[n_feat + 1 : n_feat + 1 + n_sub]
    w, sems = rest[n_feat + 1 + n_sub :]
    step = w.shape[1] // chunks
    copies = []
    for c in range(chunks):
        at = pl.ds(c * step, step)
        copies.append(pltpu.make_async_copy(w_hbm.at[:, at], w.at[:, at], sems.at[c]))
        copies[-1].start()
    me = lax.axis_index("feat")
    head = lax.axis_index("sub")
    rows_dev = slot_count * DRAFT
    rows = n_feat * rows_dev
    rows_out = out_refs[0].shape[0]
    tokens = n_sub * rows_out
    owners, slots = slot_of(owner_ref, head, requests)
    row = lax.broadcasted_iota(jnp.int32, (tokens, rows), 0)
    col = lax.broadcasted_iota(jnp.int32, (tokens, rows), 1)
    token = (row // rows_out ^ head) * rows_out + row % rows_out
    wanted = jnp.full((tokens, rows), -1, jnp.int32)
    for r in range(requests):
        start = ((owners[r] ^ me) * slot_count + slots[r]) * DRAFT
        wanted = jnp.where(token // DRAFT == r, start + token % DRAFT, wanted)
    picks = jnp.where(wanted == col, 1.0, 0.0).astype(jnp.bfloat16)
    held = jnp.concatenate([ref[...].astype(jnp.float32) for ref in att_refs], axis=0)
    x = jnp.dot(picks, held.astype(jnp.bfloat16), preferred_element_type=jnp.float32).astype(
        jnp.bfloat16
    )
    for c in range(chunks):
        copies[c].wait()
        at = slice(c * step, (c + 1) * step)
        y = jnp.dot(x, w[:, at], preferred_element_type=jnp.float32)
        for k in range(n_sub):
            out_refs[k][:, at] = y[k * rows_out : (k + 1) * rows_out].astype(jnp.bfloat16)


SMEM = pl.BlockSpec(memory_space=pltpu.SMEM)
VMEM = pl.BlockSpec(memory_space=pltpu.VMEM)
ANY = pl.BlockSpec(memory_space=pl.ANY)
MIB = 1 << 20


def body(
    hidden,
    input_norm_gain,
    query_weight,
    key_weight,
    value_weight,
    adapter_down_weight,
    adapter_up_weight,
    output_weight,
    request_adapter,
    stored_owner,
    stored_lengths,
    stored_keys,
    stored_values,
):
    n_feat = lax.axis_size("feat")
    n_sub = lax.axis_size("sub")
    tokens, features = hidden.shape
    query_cols = query_weight.shape[1]
    head_dim = key_weight.shape[1]
    slot_count, context, _ = stored_keys.shape
    requests = request_adapter.shape[0]
    rows_dev = slot_count * DRAFT
    down_cols = adapter_down_weight.shape[1]
    out_cols = output_weight.shape[1]
    block_cols = query_cols + 2 * head_dim + 2 * LANES
    bf16 = jnp.bfloat16
    f32 = jnp.float32

    chunks = 4
    *parts, rot = pl.pallas_call(
        functools.partial(project_kernel, n_feat, slot_count, requests, chunks),
        out_shape=[jax.ShapeDtypeStruct((rows_dev, block_cols), f32)] * n_feat
        + [jax.ShapeDtypeStruct((rows_dev, 2 * LANES), f32)],
        in_specs=[SMEM] * 3 + [VMEM] * 2 + [ANY] * 4,
        out_specs=[VMEM] * (n_feat + 1),
        scratch_shapes=[
            pltpu.VMEM((features, query_cols), bf16),
            pltpu.VMEM((features, head_dim), bf16),
            pltpu.VMEM((features, head_dim), bf16),
            pltpu.VMEM((features, down_cols), bf16),
            pltpu.VMEM((n_feat * rows_dev, query_cols + 2 * head_dim + down_cols), f32),
            pltpu.SemaphoreType.DMA((chunks, 4)),
        ],
        compiler_params=pltpu.CompilerParams(vmem_limit_bytes=24 * MIB),
        name="project",
    )(
        stored_owner,
        request_adapter,
        stored_lengths,
        hidden,
        input_norm_gain.reshape(1, features),
        query_weight,
        key_weight,
        value_weight,
        adapter_down_weight,
    )

    def spread(blocks, axis, size):
        got = [blocks[0]]
        for k in range(1, size):
            got.append(lax.ppermute(blocks[k], axis, [(i, i ^ k) for i in range(size)]))
        return got

    parts = spread(parts, "feat", n_feat)
    chunks = 8
    attended = pl.pallas_call(
        functools.partial(
            attend_kernel, n_feat, slot_count, requests, n_feat * features, chunks
        ),
        out_shape=jax.ShapeDtypeStruct((rows_dev, query_cols), bf16),
        in_specs=[SMEM] * 3 + [VMEM] * (n_feat + 1) + [ANY] * 3,
        out_specs=VMEM,
        scratch_shapes=[
            pltpu.VMEM((slot_count, LANES, query_cols), bf16),
            pltpu.VMEM(stored_keys.shape, bf16),
            pltpu.VMEM(stored_values.shape, bf16),
            pltpu.VMEM((rows_dev * query_cols // head_dim, context), f32),
            pltpu.SemaphoreType.DMA((2, chunks)),
            pltpu.SemaphoreType.DMA((slot_count,)),
        ],
        compiler_params=pltpu.CompilerParams(vmem_limit_bytes=24 * MIB),
        name="attend",
    )(
        stored_owner,
        request_adapter,
        stored_lengths,
        rot,
        *parts,
        adapter_up_weight,
        stored_keys,
        stored_values,
    )
    held = spread([attended] * n_feat, "feat", n_feat)
    chunks = 4
    outs = pl.pallas_call(
        functools.partial(output_kernel, n_feat, n_sub, slot_count, requests, chunks),
        out_shape=[jax.ShapeDtypeStruct((tokens // n_sub, out_cols), bf16)] * n_sub,
        in_specs=[SMEM] + [VMEM] * n_feat + [ANY],
        out_specs=[VMEM] * n_sub,
        scratch_shapes=[
            pltpu.VMEM(output_weight.shape, bf16),
            pltpu.SemaphoreType.DMA((chunks,)),
        ],
        compiler_params=pltpu.CompilerParams(vmem_limit_bytes=16 * MIB),
        name="output",
    )(stored_owner, *held, output_weight)
    outs = spread(outs, "sub", n_sub)
    total = outs[0].astype(f32)
    for part in outs[1:]:
        total = total + part.astype(f32)
    return total.astype(bf16)


def solution(mesh):
    in_specs = (
        P("groups", "feat"),
        P("feat"),
        P("feat", "sub"),
        P("feat", "sub"),
        P("feat", "sub"),
        P("feat", None),
        P(None, "sub"),
        P("sub", "feat"),
        P("groups"),
        P("groups", None),
        P("groups"),
        P(("groups", "feat"), None, "sub"),
        P(("groups", "feat"), None, "sub"),
    )
    out_specs = P(("groups", "sub"), "feat")
    return jax.shard_map(body, mesh=mesh, in_specs=in_specs, out_specs=out_specs, check_vma=False)
```

time: 107 us -> 48 us (0.45)
  waiting for transfers between devices: 45.5 us -> 11.7 us
  blocking collectives: 19.5 us -> 0 us
  matrix products: 17.2 us -> 0 us
  between operations: 14.3 us -> 0.05 us
  Pallas kernels: 0 us -> 13.8 us
  starting transfers between devices: 0.04 us -> 9.55 us
  local copies, waits for them, and re-layouts: 4.35 us -> 11.9 us
  other arithmetic: 5.08 us -> 0.63 us
    unnamed x3 -> x0, waiting for transfers between devices: 33.2 us -> none
    dot_general x12 -> x0, matrix products: 17.2 us -> none  [the longest x1 3.9 us: body(): jnp.einsum('sdgx,scx->sdgc', query, stored_keys, preferred_element_type=j...]
    psum x2 -> x0, blocking collectives: 14.3 us -> none  [the longest x1 8.39 us: body(): squares = lax.psum(jnp.sum(hidden32 * hidden32, axis=1), 'feat')]
    pallas_call x0 -> x3, Pallas kernels: none -> 13.8 us  [the longest x1 6.25 us: body(): pl.pallas_call(functools.partial(attend_kernel, n_feat, slot_count, reque...]
    reduce_scatter x1 -> x0, waiting for transfers between devices: 12.2 us -> none  [body(): lax.psum_scatter(jnp.concatenate([query_part, key_part, value_part], axis...]
    ppermute x0 -> x9, waiting for transfers between devices: none -> 11.7 us  [spread(): got.append(lax.ppermute(blocks[k], axis, [(i, i ^ k) for i in range(size)]))]
    ppermute x0 -> x9, starting transfers between devices: none -> 9.55 us  [spread(): got.append(lax.ppermute(blocks[k], axis, [(i, i ^ k) for i in range(size)]))]
    unnamed x17 -> x24, local copies, waits for them, and re-layouts: 2 us -> 11.1 us
  transfers between devices with their start and end apart: 2 -> 9, of which waited for: 2 -> 6; matrix products, arithmetic and copies ran while one was open for 2% -> 0% of each run, Pallas kernels for 0% -> 0%
where the time goes in v1:
time: 48 us; the launch traced here: 47.7 us
  Pallas kernels  13.8 us (29%)
  local copies, waits for them, and re-layouts  11.9 us (25%)
  waiting for transfers between devices  11.7 us (24%)
  starting transfers between devices  9.55 us (20%)
  other arithmetic  0.63 us (1%)
    ppermute x9, waiting for transfers between devices, spread(): got.append(lax.ppermute(blocks[k], axis, [(i, i ^ k) for i in range(size)]))  11.7 us
    unnamed x24, local copies, waits for them, and re-layouts  11.1 us
    ppermute x9, starting transfers between devices, spread(): got.append(lax.ppermute(blocks[k], axis, [(i, i ^ k) for i in range(size)]))  9.55 us
    pallas_call x1, Pallas kernels, body(): pl.pallas_call(functools.partial(attend_kernel, n_feat, slot_count, reque...  6.25 us
    pallas_call x1, Pallas kernels, body(): pl.pallas_call(functools.partial(project_kernel, n_feat, slot_count, requ...  5.24 us
    pallas_call x1, Pallas kernels, body(): pl.pallas_call(functools.partial(output_kernel, n_feat, n_sub, slot_count...  2.32 us
  transfers between devices with their start and end apart: 9, of which 6 were waited for; matrix products, arithmetic and copies ran while one was open for 0% of the time, Pallas kernels for 0%

profile of v1, /device:TPU:0, one launch (start us, length us, event | category | flops | bytes accessed | tf_op | source)
XLA Modules:
  0.0 47.7 jit_solution(1358515913176298223)
XLA Ops:
  0.0 0.8 %reshape.3.gain_ref = bf16[1,2048]{1,0:T(2,128)(2,1)S(1)} reshape(bf16[2048]{0:T(1024)(128)(2,1)} %param.14) | data formatting | bytes 8192 | tf_op jit(solution)/shard_map/reshape | solution.py:353
  0.8 2.4 %copy-done.2 = bf16[2048,1024]{1,0:T(8,128)(2,1)S(1)} copy-done((bf16[2048,1024]{1,0:T(8,128)(2,1)S(1)}, bf16[2048,1024]{1,0:T(8,128)(2,1)}, u32[]{:S(2)}) %copy-start.2) | copy-done | bytes 4194328
  3.2 1.6 %copy-done.4 = bf16[2048,512]{1,0:T(8,128)(2,1)S(1)} copy-done((bf16[2048,512]{1,0:T(8,128)(2,1)S(1)}, bf16[2048,512]{1,0:T(8,128)(2,1)}, u32[]{:S(2)}) %copy-start.4) | copy-done | bytes 2097176
  4.8 1.0 %copy-done.6 = bf16[2048,128]{1,0:T(8,128)(2,1)S(1)} copy-done((bf16[2048,128]{1,0:T(8,128)(2,1)S(1)}, bf16[2048,128]{1,0:T(8,128)(2,1)}, u32[]{:S(2)}) %copy-start.6) | copy-done | bytes 524312
  5.9 1.0 %copy-done.7 = bf16[2048,128]{1,0:T(8,128)(2,1)S(1)} copy-done((bf16[2048,128]{1,0:T(8,128)(2,1)S(1)}, bf16[2048,128]{1,0:T(8,128)(2,1)}, u32[]{:S(2)}) %copy-start.7) | copy-done | bytes 524312
  6.9 0.8 %copy-done.8 = bf16[16,2048]{1,0:T(8,128)(2,1)S(1)} copy-done((bf16[16,2048]{1,0:T(8,128)(2,1)S(1)}, bf16[16,2048]{1,0:T(8,128)(2,1)}, u32[]{:S(2)}) %copy-start.8) | copy-done | bytes 65560
  7.7 0.7 %copy-done.9 = s32[4,4]{1,0:T(4,128)S(1)} copy-done((s32[4,4]{1,0:T(4,128)S(1)}, s32[4,4]{1,0:T(4,128)}, u32[]{:S(2)}) %copy-start.9) | copy-done | bytes 88
  8.4 0.7 %copy-done.10 = s32[4]{0:T(128)S(1)} copy-done((s32[4]{0:T(128)S(1)}, s32[4]{0:T(128)}, u32[]{:S(2)}) %copy-start.10) | copy-done | bytes 40
  9.1 0.7 %copy-done.11 = s32[4]{0:T(128)S(1)} copy-done((s32[4]{0:T(128)S(1)}, s32[4]{0:T(128)}, u32[]{:S(2)}) %copy-start.11) | copy-done | bytes 40
  9.7 5.2 %project.1 = (f32[8,1536]{1,0:T(8,128)S(1)}, f32[8,1536]{1,0:T(8,128)S(1)}, f32[8,1536]{1,0:T(8,128)S(1)}, f32[8,1536]{1,0:T(8,128)S(1)}, f32[8,256]{1,0:T(8,128)S(1)}) custom-call(s32[4,4]{1,0:T(4,128)S(1)} %copy-done.9, s32[4]{0:T(128)S(1)} %copy-done.10, s32[4]{0:T(128)S(1)} %copy-done.11, bf16[16,2048]{1,0:T(8,128)(2,1)S(1)} %copy-done.8, ...), custom_call_target="tpu_custom_call" | custom-call | tf_op jit(solution)/shard_map/project/pallas_call | solution.py:332
  15.0 0.6 %collective-permute-start = (f32[8,1536]{1,0:T(8,128)S(1)}, f32[8,1536]{1,0:T(8,128)S(1)}, u32[]{:S(2)}, u32[]{:S(2)}) collective-permute-start(f32[8,1536]{1,0:T(8,128)S(1)} %get-tuple-element.16), channel_id=1, source_target_pairs={{0,4},{4,0},{8,12},{12,8},{1,5},{5,1},{9,13},{13,9},{2,6},{6,2},{1... | collective-permute-start | bytes 147464 | tf_op jit(solution)/shard_map/ppermute | solution.py:363
  15.5 2.6 %collective-permute-start.1 = (f32[8,1536]{1,0:T(8,128)S(1)}, f32[8,1536]{1,0:T(8,128)S(1)}, u32[]{:S(2)}, u32[]{:S(2)}) collective-permute-start(f32[8,1536]{1,0:T(8,128)S(1)} %get-tuple-element.17), channel_id=1, source_target_pairs={{0,8},{4,12},{8,0},{12,4},{1,9},{5,13},{9,1},{13,5},{2,10},{6,14},... | collective-permute-start | bytes 147464 | tf_op jit(solution)/shard_map/ppermute | solution.py:363
  18.1 0.0 collective-permute-start.2
  18.2 0.0 collective-permute-done.rest_1_
  18.2 2.3 %collective-permute-done.1.rest_2_ = f32[8,1536]{1,0:T(8,128)S(1)} collective-permute-done((f32[8,1536]{1,0:T(8,128)S(1)}, f32[8,1536]{1,0:T(8,128)S(1)}, u32[]{:S(2)}, u32[]{:S(2)}) %collective-permute-start.1) | collective-permute-done | bytes 49184 | tf_op jit(solution)/shard_map/ppermute | solution.py:363
  20.5 1.4 %collective-permute-done.2.rest_3_ = f32[8,1536]{1,0:T(8,128)S(1)} collective-permute-done((f32[8,1536]{1,0:T(8,128)S(1)}, f32[8,1536]{1,0:T(8,128)S(1)}, u32[]{:S(2)}, u32[]{:S(2)}) %collective-permute-start.2) | collective-permute-done | bytes 49184 | tf_op jit(solution)/shard_map/ppermute | solution.py:363
  21.8 2.2 %copy-done.1 = bf16[2,8192,128]{2,1,0:T(8,128)(2,1)S(1)} copy-done((bf16[2,8192,128]{2,1,0:T(8,128)(2,1)S(1)}, bf16[2,8192,128]{2,1,0:T(8,128)(2,1)}, u32[]{:S(2)}) %copy-start.1) | copy-done | bytes 4194328
  24.0 6.3 %attend.1.rest_0_ = bf16[8,1024]{1,0:T(8,128)(2,1)S(1)} custom-call(s32[4,4]{1,0:T(4,128)S(1)} %copy-done.9, s32[4]{0:T(128)S(1)} %copy-done.10, s32[4]{0:T(128)S(1)} %copy-done.11, f32[8,256]{1,0:T(8,128)S(1)} %get-tuple-element.14.rot_ref, f32[8,1536]{1,0:T(8,128)S(1)} %get-tuple-element.15.rest_0_, f32[8,1536]{1,0:T(8,128)S(1)} %collective-permute-done.rest_1_, ...), custom_call_target="tpu_custom_call" | custom-call | tf_op jit(solution)/shard_map/attend/pallas_call | solution.py:368
  30.3 0.9 %collective-permute-start.5 = (bf16[8,1024]{1,0:T(8,128)(2,1)S(1)}, bf16[8,1024]{1,0:T(8,128)(2,1)S(1)}, u32[]{:S(2)}, u32[]{:S(2)}) collective-permute-start(bf16[8,1024]{1,0:T(8,128)(2,1)S(1)} %attend.1.rest_0_), channel_id=1, source_target_pairs={{0,12},{4,8},{8,4},{12,0},{1,13},{5,9},{9,5},{13,1},{2,14},{6,10},... | collective-permute-start | bytes 49160 | tf_op jit(solution)/shard_map/ppermute | solution.py:363
  31.2 0.9 %collective-permute-start.4 = (bf16[8,1024]{1,0:T(8,128)(2,1)S(1)}, bf16[8,1024]{1,0:T(8,128)(2,1)S(1)}, u32[]{:S(2)}, u32[]{:S(2)}) collective-permute-start(bf16[8,1024]{1,0:T(8,128)(2,1)S(1)} %attend.1.rest_0_), channel_id=1, source_target_pairs={{0,8},{4,12},{8,0},{12,4},{1,9},{5,13},{9,1},{13,5},{2,10},{6,14},... | collective-permute-start | bytes 49160 | tf_op jit(solution)/shard_map/ppermute | solution.py:363
  32.1 0.1 collective-permute-start.3
  32.2 1.3 %collective-permute-done.5.rest_3_ = bf16[8,1024]{1,0:T(8,128)(2,1)S(1)} collective-permute-done((bf16[8,1024]{1,0:T(8,128)(2,1)S(1)}, bf16[8,1024]{1,0:T(8,128)(2,1)S(1)}, u32[]{:S(2)}, u32[]{:S(2)}) %collective-permute-start.5) | collective-permute-done | bytes 16416 | tf_op jit(solution)/shard_map/ppermute | solution.py:363
  33.5 1.4 %collective-permute-done.4.rest_2_ = bf16[8,1024]{1,0:T(8,128)(2,1)S(1)} collective-permute-done((bf16[8,1024]{1,0:T(8,128)(2,1)S(1)}, bf16[8,1024]{1,0:T(8,128)(2,1)S(1)}, u32[]{:S(2)}, u32[]{:S(2)}) %collective-permute-start.4) | collective-permute-done | bytes 16416 | tf_op jit(solution)/shard_map/ppermute | solution.py:363
  34.9 0.0 collective-permute-done.3.rest_1_
  34.9 2.3 %output.1 = (bf16[4,2048]{1,0:T(4,128)(2,1)S(1)}, bf16[4,2048]{1,0:T(4,128)(2,1)S(1)}, bf16[4,2048]{1,0:T(4,128)(2,1)S(1)}, bf16[4,2048]{1,0:T(4,128)(2,1)S(1)}) custom-call(s32[4,4]{1,0:T(4,128)S(1)} %copy-done.9, bf16[8,1024]{1,0:T(8,128)(2,1)S(1)} %attend.1.rest_0_, bf16[8,1024]{1,0:T(8,128)(2,1)S(1)} %collective-permute-done.3.rest_1_, ...), custom_call_target="tpu_custom_call" | custom-call | tf_op jit(solution)/shard_map/output/pallas_call | solution.py:397
  37.3 1.6 %collective-permute-start.6 = (bf16[4,2048]{1,0:T(4,128)(2,1)S(1)}, bf16[4,2048]{1,0:T(4,128)(2,1)S(1)}, u32[]{:S(2)}, u32[]{:S(2)}) collective-permute-start(bf16[4,2048]{1,0:T(4,128)(2,1)S(1)} %get-tuple-element.20), channel_id=1, source_target_pairs={{0,1},{1,0},{2,3},{3,2},{4,5},{5,4},{6,7},{7,6},{8,9},{9,8},{10,11... | collective-permute-start | bytes 49160 | tf_op jit(solution)/shard_map/ppermute | solution.py:363
  38.9 2.6 %collective-permute-start.7 = (bf16[4,2048]{1,0:T(4,128)(2,1)S(1)}, bf16[4,2048]{1,0:T(4,128)(2,1)S(1)}, u32[]{:S(2)}, u32[]{:S(2)}) collective-permute-start(bf16[4,2048]{1,0:T(4,128)(2,1)S(1)} %get-tuple-element.21), channel_id=1, source_target_pairs={{0,2},{1,3},{2,0},{3,1},{4,6},{5,7},{6,4},{7,5},{8,10},{9,11},{10,... | collective-permute-start | bytes 49160 | tf_op jit(solution)/shard_map/ppermute | solution.py:363
  41.5 0.2 collective-permute-start.8
  41.7 0.0 collective-permute-done.6
  41.7 1.9 %collective-permute-done.7 = bf16[4,2048]{1,0:T(4,128)(2,1)S(1)} collective-permute-done((bf16[4,2048]{1,0:T(4,128)(2,1)S(1)}, bf16[4,2048]{1,0:T(4,128)(2,1)S(1)}, u32[]{:S(2)}, u32[]{:S(2)}) %collective-permute-start.7) | collective-permute-done | bytes 16416 | tf_op jit(solution)/shard_map/ppermute | solution.py:363
  43.6 3.4 %collective-permute-done.8 = bf16[4,2048]{1,0:T(4,128)(2,1)S(1)} collective-permute-done((bf16[4,2048]{1,0:T(4,128)(2,1)S(1)}, bf16[4,2048]{1,0:T(4,128)(2,1)S(1)}, u32[]{:S(2)}, u32[]{:S(2)}) %collective-permute-start.8) | collective-permute-done | bytes 16416 | tf_op jit(solution)/shard_map/ppermute | solution.py:363
  47.0 0.6 %add_convert_fusion = bf16[4,2048]{1,0:T(4,128)(2,1)} fusion(bf16[4,2048]{1,0:T(4,128)(2,1)S(1)} %collective-permute-done.8, bf16[4,2048]{1,0:T(4,128)(2,1)S(1)} %collective-permute-done.7, bf16[4,2048]{1,0:T(4,128)(2,1)S(1)} %collective-permute-done.6, bf16[4,2048]{1,0:T(4,128)(2,1)S(1)} %get-tuple-element.19), kind=kLoop, calls=%fused_computation | loop fusion | flops 65536 | bytes 81920 | tf_op jit(solution)/shard_map/convert_element_type | solution.py:413
  (15 shorter events, 0.0 us)
Async XLA Ops:
  0.0 21.8 %copy-start = (bf16[2,8192,128]{2,1,0:T(8,128)(2,1)S(1)}, bf16[2,8192,128]{2,1,0:T(8,128)(2,1)}, u32[]{:S(2)}) copy-start(bf16[2,8192,128]{2,1,0:T(8,128)(2,1)} %rest_5_.1) | copy-start | bytes 12582916
  0.8 2.4 %copy-start.2 = (bf16[2048,1024]{1,0:T(8,128)(2,1)S(1)}, bf16[2048,1024]{1,0:T(8,128)(2,1)}, u32[]{:S(2)}) copy-start(bf16[2048,1024]{1,0:T(8,128)(2,1)} %wq_hbm.1) | copy-start | bytes 12582916
  3.2 1.6 %copy-start.4 = (bf16[2048,512]{1,0:T(8,128)(2,1)S(1)}, bf16[2048,512]{1,0:T(8,128)(2,1)}, u32[]{:S(2)}) copy-start(bf16[2048,512]{1,0:T(8,128)(2,1)} %wd_hbm.1) | copy-start | bytes 6291460
  4.8 1.0 %copy-start.6 = (bf16[2048,128]{1,0:T(8,128)(2,1)S(1)}, bf16[2048,128]{1,0:T(8,128)(2,1)}, u32[]{:S(2)}) copy-start(bf16[2048,128]{1,0:T(8,128)(2,1)} %wk_hbm.1) | copy-start | bytes 1572868
  5.9 1.0 %copy-start.7 = (bf16[2048,128]{1,0:T(8,128)(2,1)S(1)}, bf16[2048,128]{1,0:T(8,128)(2,1)}, u32[]{:S(2)}) copy-start(bf16[2048,128]{1,0:T(8,128)(2,1)} %wv_hbm.1) | copy-start | bytes 1572868
  6.9 0.8 %copy-start.8 = (bf16[16,2048]{1,0:T(8,128)(2,1)S(1)}, bf16[16,2048]{1,0:T(8,128)(2,1)}, u32[]{:S(2)}) copy-start(bf16[16,2048]{1,0:T(8,128)(2,1)} %hidden_ref.1) | copy-start | bytes 196612
  7.7 0.7 %copy-start.9 = (s32[4,4]{1,0:T(4,128)S(1)}, s32[4,4]{1,0:T(4,128)}, u32[]{:S(2)}) copy-start(s32[4,4]{1,0:T(4,128)} %owner_ref.5) | copy-start | bytes 196
  8.4 0.7 %copy-start.10 = (s32[4]{0:T(128)S(1)}, s32[4]{0:T(128)}, u32[]{:S(2)}) copy-start(s32[4]{0:T(128)} %adapter_ref.3) | copy-start | bytes 52
  9.1 0.7 %copy-start.11 = (s32[4]{0:T(128)S(1)}, s32[4]{0:T(128)}, u32[]{:S(2)}) copy-start(s32[4]{0:T(128)} %lengths_ref.3) | copy-start | bytes 52
  9.7 12.1 %copy-start.5 = (bf16[512,1024]{1,0:T(8,128)(2,1)S(1)}, bf16[512,1024]{1,0:T(8,128)(2,1)}, u32[]{:S(2)}) copy-start(bf16[512,1024]{1,0:T(8,128)(2,1)} %rest_4_.2) | copy-start | bytes 3145732
  15.0 3.2 %collective-permute-start = (f32[8,1536]{1,0:T(8,128)S(1)}, f32[8,1536]{1,0:T(8,128)S(1)}, u32[]{:S(2)}, u32[]{:S(2)}) collective-permute-start(f32[8,1536]{1,0:T(8,128)S(1)} %get-tuple-element.16), channel_id=1, source_target_pairs={{0,4},{4,0},{8,12},{12,8},{1,5},{5,1},{9,13},{13,9},{2,6},{6,2},{1... | collective-permute-start | bytes 147464 | tf_op jit(solution)/shard_map/ppermute | solution.py:363
  15.5 4.9 %collective-permute-start.1 = (f32[8,1536]{1,0:T(8,128)S(1)}, f32[8,1536]{1,0:T(8,128)S(1)}, u32[]{:S(2)}, u32[]{:S(2)}) collective-permute-start(f32[8,1536]{1,0:T(8,128)S(1)} %get-tuple-element.17), channel_id=1, source_target_pairs={{0,8},{4,12},{8,0},{12,4},{1,9},{5,13},{9,1},{13,5},{2,10},{6,14},... | collective-permute-start | bytes 147464 | tf_op jit(solution)/shard_map/ppermute | solution.py:363
  18.1 3.7 %collective-permute-start.2 = (f32[8,1536]{1,0:T(8,128)S(1)}, f32[8,1536]{1,0:T(8,128)S(1)}, u32[]{:S(2)}, u32[]{:S(2)}) collective-permute-start(f32[8,1536]{1,0:T(8,128)S(1)} %get-tuple-element.18), channel_id=1, source_target_pairs={{0,12},{4,8},{8,4},{12,0},{1,13},{5,9},{9,5},{13,1},{2,14},{6,10},... | collective-permute-start | bytes 147464 | tf_op jit(solution)/shard_map/ppermute | solution.py:363
  21.8 2.2 %copy-start.1 = (bf16[2,8192,128]{2,1,0:T(8,128)(2,1)S(1)}, bf16[2,8192,128]{2,1,0:T(8,128)(2,1)}, u32[]{:S(2)}) copy-start(bf16[2,8192,128]{2,1,0:T(8,128)(2,1)} %rest_6_.1) | copy-start | bytes 12582916
  24.0 10.9 %copy-start.3 = (bf16[1024,2048]{1,0:T(8,128)(2,1)S(1)}, bf16[1024,2048]{1,0:T(8,128)(2,1)}, u32[]{:S(2)}) copy-start(bf16[1024,2048]{1,0:T(8,128)(2,1)} %rest_4_.3) | copy-start | bytes 12582916
  30.3 3.2 %collective-permute-start.5 = (bf16[8,1024]{1,0:T(8,128)(2,1)S(1)}, bf16[8,1024]{1,0:T(8,128)(2,1)S(1)}, u32[]{:S(2)}, u32[]{:S(2)}) collective-permute-start(bf16[8,1024]{1,0:T(8,128)(2,1)S(1)} %attend.1.rest_0_), channel_id=1, source_target_pairs={{0,12},{4,8},{8,4},{12,0},{1,13},{5,9},{9,5},{13,1},{2,14},{6,10},... | collective-permute-start | bytes 49160 | tf_op jit(solution)/shard_map/ppermute | solution.py:363
  31.2 3.7 %collective-permute-start.4 = (bf16[8,1024]{1,0:T(8,128)(2,1)S(1)}, bf16[8,1024]{1,0:T(8,128)(2,1)S(1)}, u32[]{:S(2)}, u32[]{:S(2)}) collective-permute-start(bf16[8,1024]{1,0:T(8,128)(2,1)S(1)} %attend.1.rest_0_), channel_id=1, source_target_pairs={{0,8},{4,12},{8,0},{12,4},{1,9},{5,13},{9,1},{13,5},{2,10},{6,14},... | collective-permute-start | bytes 49160 | tf_op jit(solution)/shard_map/ppermute | solution.py:363
  32.1 2.8 %collective-permute-start.3 = (bf16[8,1024]{1,0:T(8,128)(2,1)S(1)}, bf16[8,1024]{1,0:T(8,128)(2,1)S(1)}, u32[]{:S(2)}, u32[]{:S(2)}) collective-permute-start(bf16[8,1024]{1,0:T(8,128)(2,1)S(1)} %attend.1.rest_0_), channel_id=1, source_target_pairs={{0,4},{4,0},{8,12},{12,8},{1,5},{5,1},{9,13},{13,9},{2,6},{6,2},{1... | collective-permute-start | bytes 49160 | tf_op jit(solution)/shard_map/ppermute | solution.py:363
  37.3 4.5 %collective-permute-start.6 = (bf16[4,2048]{1,0:T(4,128)(2,1)S(1)}, bf16[4,2048]{1,0:T(4,128)(2,1)S(1)}, u32[]{:S(2)}, u32[]{:S(2)}) collective-permute-start(bf16[4,2048]{1,0:T(4,128)(2,1)S(1)} %get-tuple-element.20), channel_id=1, source_target_pairs={{0,1},{1,0},{2,3},{3,2},{4,5},{5,4},{6,7},{7,6},{8,9},{9,8},{10,11... | collective-permute-start | bytes 49160 | tf_op jit(solution)/shard_map/ppermute | solution.py:363
  38.9 4.7 %collective-permute-start.7 = (bf16[4,2048]{1,0:T(4,128)(2,1)S(1)}, bf16[4,2048]{1,0:T(4,128)(2,1)S(1)}, u32[]{:S(2)}, u32[]{:S(2)}) collective-permute-start(bf16[4,2048]{1,0:T(4,128)(2,1)S(1)} %get-tuple-element.21), channel_id=1, source_target_pairs={{0,2},{1,3},{2,0},{3,1},{4,6},{5,7},{6,4},{7,5},{8,10},{9,11},{10,... | collective-permute-start | bytes 49160 | tf_op jit(solution)/shard_map/ppermute | solution.py:363
  41.5 5.5 %collective-permute-start.8 = (bf16[4,2048]{1,0:T(4,128)(2,1)S(1)}, bf16[4,2048]{1,0:T(4,128)(2,1)S(1)}, u32[]{:S(2)}, u32[]{:S(2)}) collective-permute-start(bf16[4,2048]{1,0:T(4,128)(2,1)S(1)} %get-tuple-element.22), channel_id=1, source_target_pairs={{0,3},{1,2},{2,1},{3,0},{4,7},{5,6},{6,5},{7,4},{8,11},{9,10},{10,... | collective-permute-start | bytes 49160 | tf_op jit(solution)/shard_map/ppermute | solution.py:363
